TPU v7x, 32 devices: a whole 2x2x4 slice. The times are simulated.
32 devices in a mesh: rows: 16 (over z, y, x), cols: 2 (over core).
Axes of the slice: x: 2, y: 2, z: 4, core: 2. Of those that a mesh axis runs over, the one named last changes fastest.
Arguments:
- points: bfloat16 [20480, 512], P('rows', 'cols'), may hold values from -6 to 6
- factor: bfloat16 [20480, 1024], P('rows', 'cols'), may hold values from -2 to 2
- weights: float32 [20480], P('rows'), may hold values from -4 to 4
- pivot_slots: int32 [4, 128], replicated, may hold values from 0 to 1279, as said below
- pivot_owners: int32 [4, 128], replicated, may hold values from 0 to 15
Outputs:
- new_panels: bfloat16 [20480, 512], P('rows', 'cols')
- gram_old: float32 [512, 1024], P('rows', 'cols')
- gram_new: float32 [512, 512], P('rows', 'cols')
Inputs may be any that keep to these rules, and one draw needn't show every extreme that they name: Pivot k of panel q is row pivot_slots[q,k] of the block of device pivot_owners[q,k]; the pivots of all panels together are distinct points.
All inputs are finite; a program needn't handle non-finite values.
Results may differ from a plain program's by a relative error of at most 0.009.
Values may be sent and summed in bfloat16 or wider, within the bound.
A program may use at most 64 MiB of HBM per device.

v0:
```python
import functools
import math

import jax
import jax.numpy as jnp
from jax import lax
from jax.experimental import pallas as pl
from jax.experimental.pallas import tpu as pltpu
from jax.sharding import PartitionSpec as P

RIDGE_LEVEL = 1.0
BLOCK = 8
VMEM = pltpu.VMEM
HIGH = lax.Precision.HIGHEST
NT = (((1,), (1,)), ((), ()))
TN = (((0,), (0,)), ((), ()))


def remote(src, dst, send, recv, row, col):
    return pltpu.make_async_remote_copy(
        src_ref=src, dst_ref=dst, send_sem=send, recv_sem=recv,
        device_id=(row, col), device_id_type=pl.DeviceIdType.MESH,
    )


def greet(me, col, inner, outer):
    place, layer = me % inner, me // inner
    barrier = pltpu.get_barrier_semaphore()
    peers = [(me, 1 - col)]
    peers += [(layer * inner + (place + d) % inner, col) for d in range(1, inner)]
    peers += [(((layer + d) % outer) * inner + place, col) for d in range(1, outer)]
    for peer in peers:
        pl.semaphore_signal(barrier, inc=1, device_id=peer, device_id_type=pl.DeviceIdType.MESH)
    pl.semaphore_wait(barrier, len(peers))


def factor_block(size, a, e, rows, outs, wide):
    for first in range(0, size, BLOCK):
        span = slice(first, first + BLOCK)
        strip = a[span, :]
        for k in range(BLOCK):
            wide[first // BLOCK % 2 * BLOCK + k] = jnp.broadcast_to(strip[:, first + k:first + k + 1], (BLOCK, size))
        d = {(i, k): wide[first // BLOCK % 2 * BLOCK + k, i:i + 1, :] for i in range(BLOCK) for k in range(i + 1)}
        r = [a[first + i:first + i + 1, :] for i in range(BLOCK)]
        s = [e[first + i:first + i + 1, :] for i in range(BLOCK)]
        for k in range(BLOCK):
            scale = lax.rsqrt(d[k, k])
            r[k] = r[k] * scale
            s[k] = s[k] * scale
            for i in range(k + 1, BLOCK):
                d[i, k] = d[i, k] * scale
            for i in range(k + 1, BLOCK):
                r[i] = r[i] - d[i, k] * r[k]
                s[i] = s[i] - d[i, k] * s[k]
                for m in range(k + 1, i + 1):
                    d[i, m] = d[i, m] - d[i, k] * d[m, k]
        base = BLOCK * (first // BLOCK % 2)
        for k in range(BLOCK):
            rows[base + k:base + k + 1, :] = r[k]
            e[first + k:first + k + 1, :] = s[k]
        after = first + BLOCK
        if after < size:
            upper = jnp.transpose(rows[base:base + BLOCK, :])
            for low, high in ((after, after + BLOCK), (after + BLOCK, size)):
                if low < high:
                    rest_a = a[low:high, :]
                    rest_e = e[low:high, :]
                    for k in range(BLOCK):
                        column = upper[low:high, k:k + 1]
                        rest_a = rest_a - column * rows[base + k:base + k + 1, :]
                        rest_e = rest_e - column * e[first + k:first + k + 1, :]
                    a[low:high, :] = rest_a
                    e[low:high, :] = rest_e


def panel_kernel(inner, outer, scale_by, slots, owners, points, factor, weights, own_cols, gram_old, gram_new,
                 out_ref, other_ref, level_t, gp, ga, gacc, gmid, gb, nw, na, nacc, nmid, nb,
                 ga_send, ga_recv, gb_send, gb_recv, na_send, na_recv, nb_send, nb_recv,
                 part, piv, other_points, other_factor, buf_a, buf_b, acc,
                 prow, inv, norms, a, rows, wide,
                 a_send, a_recv, b_send, b_recv, f_send, f_recv,
                 d_send, d_recv, e_send, e_recv, x_send, x_recv):
    me = lax.axis_index("rows")
    col = lax.axis_index("cols")
    place, layer = me % inner, me // inner
    panels, size = slots.shape
    here, fw = points.shape
    half = here // 2
    feats, rank = 2 * fw, 2 * factor.shape[1]
    chunk = size // inner
    f32, bf16 = jnp.float32, jnp.bfloat16
    greet(me, col, inner, outer)

    def piece(q, p):
        return pl.ds(pl.multiple_of(q * size + p * chunk, chunk), chunk)

    def turned(row):
        return jnp.transpose(jnp.broadcast_to(row, (size, size)))

    spots = lax.broadcasted_iota(jnp.int32, (size, here), 1) + me * here
    step_a = []
    for q in range(panels):
        ids = (owners[q:q + 1, :] * here + slots[q:q + 1, :]).astype(f32)
        hot = jnp.where(spots == turned(ids)[:, 0:1].astype(jnp.int32), 1.0, 0.0).astype(bf16)
        span = slice(q * size, (q + 1) * size)
        part[span, :fw] = jnp.dot(hot, points[...], preferred_element_type=f32).astype(bf16)
        part[span, fw:] = jnp.dot(hot, factor[...], preferred_element_type=f32).astype(bf16)
        for d in range(1, inner):
            p = (place + d) % inner
            c = remote(part.at[piece(q, p)], buf_a.at[q, d - 1], a_send.at[q, d - 1], a_recv.at[q, d - 1],
                       layer * inner + p, col)
            c.start()
            step_a.append(c)
    theirs = pl.ds(pl.multiple_of((1 - col) * half, 16), half)
    swap = [
        remote(points.at[theirs], other_points, x_send.at[0], x_recv.at[0], me, 1 - col),
        remote(factor.at[theirs], other_factor, x_send.at[1], x_recv.at[1], me, 1 - col),
    ]
    for c in swap:
        c.start()

    def along(q, d):
        return remote(acc.at[q], buf_b.at[q, d - 1], b_send.at[q, d - 1], b_recv.at[q, d - 1],
                      ((layer + d) % outer) * inner + place, col)

    def around(q, d):
        it = piv.at[col, piece(q, place)]
        return remote(it, it, d_send.at[q, d - 1], d_recv.at[q, d - 1], layer * inner + (place + d) % inner, col)

    def across(q, d):
        it = piv.at[col, piece(q, (place + inner - d) % inner)]
        return remote(it, it, e_send.at[q, d], e_recv.at[q, d], me, 1 - col)

    def swap_panel(q):
        span = pl.ds(pl.multiple_of(q * size, size), size)
        return remote(out_ref.at[:, span], other_ref.at[:, span], f_send.at[q], f_recv.at[q], me, 1 - col)

    def layer_sum(q):
        total = part[piece(q, place), :]
        for d in range(1, inner):
            step_a[q * (inner - 1) + d - 1].wait_recv()
            total = total + buf_a[q, d - 1]
        acc[q] = total
        for d in range(1, outer):
            along(q, d).start()

    def whole_sum(q):
        total = acc[q]
        for d in range(1, outer):
            along(q, d).wait_recv()
            total = total + buf_b[q, d - 1]
        piv[col, piece(q, place)] = total
        for d in range(1, inner):
            around(q, d).start()
        across(q, 0).start()

    def forward(q):
        for d in range(1, inner):
            around(q, d).wait_recv()
            across(q, d).start()

    for q in range(panels):
        layer_sum(q)
        if q == min(2, panels - 1):
            whole_sum(0)
    forward(0)
    for q in range(1, min(2, panels)):
        whole_sum(q)
    prow[...] = jnp.zeros_like(prow)
    out_ref[...] = jnp.zeros_like(out_ref)
    for c in swap:
        c.wait_recv()

    def norm(x, y):
        x, y = x.astype(f32), y.astype(f32)
        return jnp.sum(x * x, axis=1, keepdims=True) + jnp.sum(y * y, axis=1, keepdims=True)

    def dot(x, y):
        return lax.dot_general(x, y, NT, preferred_element_type=f32)

    mine = pl.ds(pl.multiple_of(col * half, 16), half)
    own_norm = norm(points[mine, :], other_points[...])
    own_ids = lax.broadcasted_iota(jnp.int32, (half, size), 0) + (me * here + col * half)
    same = lax.broadcasted_iota(jnp.int32, (size, size), 0) == lax.broadcasted_iota(jnp.int32, (size, size), 1)
    eye = jnp.where(same, 1.0, 0.0)

    runs = gp.shape[1]
    lines = gp.shape[3]
    width = own_cols.shape[1]
    wide_lanes = pl.ds(pl.multiple_of(col * width, 128), width)

    def gram_a(k, d):
        p = (place + d) % inner
        return remote(gp.at[k, :, p], ga.at[k, d - 1], ga_send.at[k, d - 1], ga_recv.at[k, d - 1],
                      layer * inner + p, col)

    def gram_b(k, i):
        target = k * runs + i
        slot = (layer - target + 2 * outer - 1) % outer
        return remote(gmid.at[k, i], gb.at[slot], gb_send.at[k, i], gb_recv.at[slot], target * inner + place, col)

    def gram_got(d):
        return remote(gmid.at[0, 0], gb.at[d - 1], gb_send.at[0, 0], gb_recv.at[d - 1],
                      ((layer + d) % outer) * inner + place, col)

    def new_a(d):
        p = (place + d) % inner
        return remote(nw.at[:, p], na.at[d - 1], na_send.at[d - 1], na_recv.at[d - 1], layer * inner + p, col)

    def new_b(d):
        z = (layer + d) % outer
        return remote(nmid.at[z], nb.at[d - 1], nb_send.at[d - 1], nb_recv.at[d - 1], z * inner + place, col)

    def gram_block(k):
        swap_panel(k).wait_recv()
        lanes = pl.ds(pl.multiple_of(k * size, size), size)
        for source, which in ((out_ref, col), (other_ref, 1 - col)):
            for i in range(half // size):
                level = turned(weights[pl.ds(which * (half // size) + i, 1), :])[:, 0:1]
                block = source[i * size:(i + 1) * size, lanes].astype(f32) * level
                first = pl.multiple_of(which * half + i * size, size)
                level_t[lanes, pl.ds(first, size)] = jnp.transpose(block).astype(bf16)
        block = jnp.dot(level_t[lanes, :], factor[...], preferred_element_type=f32) * scale_by
        gp[k] = block.reshape(runs, inner, lines, factor.shape[1]).astype(bf16)
        for d in range(1, inner):
            gram_a(k, d).start()

    def gram_sum(k):
        total = gp[k, :, place].astype(f32)
        for d in range(1, inner):
            gram_a(k, d).wait_recv()
            total = total + ga[k, d - 1].astype(f32)
        gacc[k] = total
        gmid[k] = total.astype(bf16)
        for i in range(runs):
            @pl.when(layer != k * runs + i)
            def _():
                gram_b(k, i).start()

    def panel(q, carry):
        for d in range(inner):
            across(q, d).wait_recv()
        span = pl.ds(pl.multiple_of(q * size, size), size)
        ps, po = piv[col, span, :], piv[1 - col, span, :]
        pnorm = norm(ps[:, :fw], po[:, :fw])
        norms[q] = jnp.transpose(jnp.broadcast_to(pnorm, (size, size)))

        def entries(xs, xo, ys, yo, ts, to, n, row_norm):
            cross = dot(xs, ts[:, :fw]) + dot(xo, to[:, :fw])
            schur = dot(ys, ts[:, fw:]) + dot(yo, to[:, fw:])
            return jnp.exp(-(n + row_norm - 2.0 * cross) / feats) + schur / (3.0 * rank)

        def earlier(k, carry):
            other = pl.ds(pl.multiple_of(k * size, size), size)
            ts, to = piv[col, other, :], piv[1 - col, other, :]
            row_norm = norms[k][0:1, :]
            m = entries(ps[:, :fw], po[:, :fw], ps[:, fw:], po[:, fw:], ts, to, pnorm, row_norm)
            m = m - dot(prow[q], prow[k])
            prow[q, :, other] = lax.dot_general(m, inv[k], NT, precision=HIGH,
                                                preferred_element_type=f32).astype(bf16)
            return carry

        lax.fori_loop(0, q, earlier, 0)
        row_norm = norms[q][0:1, :]
        a[...] = (entries(ps[:, :fw], po[:, :fw], ps[:, fw:], po[:, fw:], ps, po, pnorm, row_norm)
                  + RIDGE_LEVEL * eye - dot(prow[q], prow[q]))
        e = inv.at[q]
        e[...] = eye

        @pl.when(q + 2 < panels)
        def _():
            whole_sum(q + 2)

        @pl.when(q + 1 < panels)
        def _():
            forward(q + 1)

        @pl.when(q > 1)
        def _():
            gram_sum(q - 2)

        @pl.when(q > 0)
        def _():
            gram_block(q - 1)
        ids = owners[pl.ds(q, 1), :] * here + slots[pl.ds(q, 1), :]
        columns = (entries(points[mine, :], other_points[...], factor[mine, :], other_factor[...], ps, po,
                           own_norm, row_norm)
                   + jnp.where(own_ids == ids, RIDGE_LEVEL, 0.0) - dot(out_ref[...], prow[q]))
        factor_block(size, a, e, rows, None, wide)
        out_ref[:, span] = lax.dot_general(columns, e[...], NT, precision=HIGH,
                                           preferred_element_type=f32).astype(bf16)
        swap_panel(q).start()
        return carry

    lax.fori_loop(0, panels, panel, 0)
    if panels > 1:
        gram_sum(panels - 2)
    gram_block(panels - 1)
    for source, which in ((out_ref, col), (other_ref, 1 - col)):
        own_cols[pl.ds(pl.multiple_of(which * half, 16), half), :] = source[:, wide_lanes]
    block = jnp.dot(level_t[...], own_cols[...], preferred_element_type=f32) * scale_by
    nw[...] = block.reshape(outer, inner, lines, width).astype(bf16)
    for d in range(1, inner):
        new_a(d).start()
    gram_sum(panels - 1)
    total = nw[:, place].astype(f32)
    for d in range(1, inner):
        new_a(d).wait_recv()
        total = total + na[d - 1].astype(f32)
    nacc[...] = total
    nmid[...] = total.astype(bf16)
    for d in range(1, outer):
        new_b(d).start()
    total = gacc[layer // runs, layer % runs]
    for d in range(1, outer):
        gram_got(d).wait_recv()
        total = total + gb[d - 1].astype(f32)
    gram_old[...] = total
    total = nacc[layer]
    for d in range(1, outer):
        new_b(d).wait_recv()
        total = total + nb[d - 1].astype(f32)
    gram_new[...] = total
    for d in range(1, inner):
        new_a(d).wait_send()
    for d in range(1, outer):
        new_b(d).wait_send()
    for c in step_a + swap:
        c.wait_send()
    for q in range(panels):
        swap_panel(q).wait_send()
        for d in range(1, inner):
            gram_a(q, d).wait_send()
        for i in range(runs):
            @pl.when(layer != q * runs + i)
            def _():
                gram_b(q, i).wait_send()
        for d in range(1, outer):
            along(q, d).wait_send()
        for d in range(1, inner):
            around(q, d).wait_send()
        for d in range(inner):
            across(q, d).wait_send()


def body(points, factor, weights, pivot_slots, pivot_owners):
    here, fw = points.shape
    rank = factor.shape[1]
    panels, size = pivot_slots.shape
    rows = lax.axis_size("rows")
    count = panels * size
    chunk = count // rows
    width = fw + rank
    half = here // 2
    bf16, f32 = jnp.bfloat16, jnp.float32
    vm = pl.BlockSpec(memory_space=VMEM)
    sem = lambda *n: pltpu.SemaphoreType.DMA(n)
    limit = 60 * 1024 * 1024

    split = rows // panels if rows < panels * panels else panels
    layers = rows // split
    piece = size // split
    runs = layers // panels
    share = count // 2
    scale = size / math.sqrt(here * rows)
    return pl.pallas_call(
        functools.partial(panel_kernel, split, layers, scale),
        out_shape=(
            jax.ShapeDtypeStruct((here, share), bf16),
            jax.ShapeDtypeStruct((chunk, rank), f32),
            jax.ShapeDtypeStruct((chunk, share), f32),
        ),
        in_specs=[vm] * 5, out_specs=(vm,) * 3, name="panels",
        scratch_shapes=[
            VMEM((half, count), bf16), VMEM((half, count), bf16), VMEM((count, here), bf16),
            VMEM((panels, runs, split, chunk, rank), bf16),
            VMEM((panels, split - 1, runs, chunk, rank), bf16),
            VMEM((panels, runs, chunk, rank), f32), VMEM((panels, runs, chunk, rank), bf16),
            VMEM((layers, chunk, rank), bf16),
            VMEM((layers, split, chunk, share), bf16),
            VMEM((split - 1, layers, chunk, share), bf16),
            VMEM((layers, chunk, share), f32), VMEM((layers, chunk, share), bf16),
            VMEM((layers - 1, chunk, share), bf16),
            sem(panels, split - 1), sem(panels, split - 1), sem(panels, runs), sem(layers),
            sem(split - 1), sem(split - 1), sem(layers - 1), sem(layers - 1),
            VMEM((count, width), bf16), VMEM((2, count, width), bf16),
            VMEM((half, fw), bf16), VMEM((half, rank), bf16),
            VMEM((panels, split - 1, piece, width), bf16),
            VMEM((panels, layers - 1, piece, width), bf16),
            VMEM((panels, piece, width), bf16),
            VMEM((panels, size, count), bf16),
            VMEM((panels, size, size), f32), VMEM((panels, size, size), f32), VMEM((size, size), f32),
            VMEM((2 * BLOCK, size), f32), VMEM((2 * BLOCK, BLOCK, size), f32),
            sem(panels, split - 1), sem(panels, split - 1), sem(panels, layers - 1), sem(panels, layers - 1),
            sem(panels), sem(panels), sem(panels, split - 1), sem(panels, split - 1),
            sem(panels, split), sem(panels, split), sem(2), sem(2),
        ],
        compiler_params=pltpu.CompilerParams(collective_id=0, has_side_effects=True, vmem_limit_bytes=limit),
    )(pivot_slots, pivot_owners, points, factor, weights.reshape(here // size, size))


def solution(mesh):
    return jax.shard_map(
        body,
        mesh=mesh,
        in_specs=(P("rows", "cols"), P("rows", "cols"), P("rows"), P(), P()),
        out_specs=(P("rows", "cols"), P("rows", "cols"), P("rows", "cols")),
        check_vma=False,
    )
```

profile of v0, /device:TPU:0, one launch (start us, length us, event | category | flops | bytes accessed | tf_op | source)
XLA Modules:
  0.0 81.9 jit_solution(16690275057398191451)
XLA Ops:
  0.6 78.0 %panels.1 = (bf16[1280,256]{1,0:T(8,128)(2,1)}, f32[32,512]{1,0:T(8,128)}, f32[32,256]{1,0:T(8,128)}) custom-call(s32[4,128]{1,0:T(4,128)} %slots.1, s32[4,128]{1,0:T(4,128)} %owners.1, bf16[1280,256]{1,0:T(8,128)(2,1)} %points.1, bf16[1280,512]{1,0:T(8,128)(2,1)} %factor.1, f32[10,128]{1,0:T(8,128)} %bitcast.1), custom_call_target="tpu_custom_call" | custom-call | tf_op jit(solution)/shard_map/panels/pallas_call | solution.py:366
  78.7 0.0 copy-start
  78.7 0.0 copy-start.1
  78.7 2.0 %copy.11 = bf16[1280,256]{1,0:T(8,128)(2,1)} copy(bf16[1280,256]{1,0:T(8,128)(2,1)} %get-tuple-element.6) | data formatting | bytes 1310720
  80.7 0.0 copy-done
  80.7 0.6 copy.12
  81.3 0.0 copy-done.1
  81.3 0.6 copy.13
Async XLA Ops:
  78.7 2.0 %copy-start = (f32[32,512]{1,0:T(8,128)S(1)}, f32[32,512]{1,0:T(8,128)}, u32[]{:S(2)}) copy-start(f32[32,512]{1,0:T(8,128)} %get-tuple-element.7) | copy-start | bytes 196612
  78.7 2.6 %copy-start.1 = (f32[32,256]{1,0:T(8,128)S(1)}, f32[32,256]{1,0:T(8,128)}, u32[]{:S(2)}) copy-start(f32[32,256]{1,0:T(8,128)} %get-tuple-element.8) | copy-start | bytes 98308
where the time goes:
time: 82.1 us; the launch traced here: 81.9 us
  Pallas kernels  78 us (95%)
  local copies, waits for them, and re-layouts  3.25 us (4%)
    pallas_call x1, Pallas kernels, body(): pl.pallas_call(functools.partial(panel_kernel, split, layers, scale), out...  78 us
    unnamed x7, local copies, waits for them, and re-layouts  3.25 us

commit v1 on v0

--- a/solution.py
+++ b/solution.py
@@ -23,19 +23,18 @@
     )
 
 
-def greet(me, col, inner, outer):
+def peers_of(me, col, inner, outer):
     place, layer = me % inner, me // inner
-    barrier = pltpu.get_barrier_semaphore()
     peers = [(me, 1 - col)]
     peers += [(layer * inner + (place + d) % inner, col) for d in range(1, inner)]
     peers += [(((layer + d) % outer) * inner + place, col) for d in range(1, outer)]
-    for peer in peers:
-        pl.semaphore_signal(barrier, inc=1, device_id=peer, device_id_type=pl.DeviceIdType.MESH)
-    pl.semaphore_wait(barrier, len(peers))
-
-
-def factor_block(size, a, e, rows, outs, wide):
+    return peers
+
+
+def factor_block(size, a, e, rows, wide, hooks):
     for first in range(0, size, BLOCK):
+        if first in hooks:
+            hooks[first]()
         span = slice(first, first + BLOCK)
         strip = a[span, :]
         for k in range(BLOCK):
@@ -73,11 +72,11 @@
                     e[low:high, :] = rest_e
 
 
-def panel_kernel(inner, outer, scale_by, slots, owners, points, factor, weights, own_cols, gram_old, gram_new,
+def panel_kernel(inner, outer, scale_by, slots, owners, points_in, factor_in, weights, own_cols, gram_old, gram_new,
                  out_ref, other_ref, level_t, gp, ga, gacc, gmid, gb, nw, na, nacc, nmid, nb,
                  ga_send, ga_recv, gb_send, gb_recv, na_send, na_recv, nb_send, nb_recv,
-                 part, piv, other_points, other_factor, buf_a, buf_b, acc,
-                 prow, inv, norms, a, rows, wide,
+                 points, factor, load, part, piv, other_points, other_factor, buf_a, buf_b, acc,
+                 prow, inv, norms, a, early, ready, columns, rows, wide,
                  a_send, a_recv, b_send, b_recv, f_send, f_recv,
                  d_send, d_recv, e_send, e_recv, x_send, x_recv):
     me = lax.axis_index("rows")
@@ -89,7 +88,17 @@
     feats, rank = 2 * fw, 2 * factor.shape[1]
     chunk = size // inner
     f32, bf16 = jnp.float32, jnp.bfloat16
-    greet(me, col, inner, outer)
+
+    loads = [
+        pltpu.make_async_copy(points_in, points, load.at[0]),
+        pltpu.make_async_copy(factor_in, factor, load.at[1]),
+    ]
+    for c in loads:
+        c.start()
+    barrier = pltpu.get_barrier_semaphore()
+    peers = peers_of(me, col, inner, outer)
+    for peer in peers:
+        pl.semaphore_signal(barrier, inc=1, device_id=peer, device_id_type=pl.DeviceIdType.MESH)
 
     def piece(q, p):
         return pl.ds(pl.multiple_of(q * size + p * chunk, chunk), chunk)
@@ -98,26 +107,18 @@
         return jnp.transpose(jnp.broadcast_to(row, (size, size)))
 
     spots = lax.broadcasted_iota(jnp.int32, (size, here), 1) + me * here
-    step_a = []
-    for q in range(panels):
+
+    def gather(q):
         ids = (owners[q:q + 1, :] * here + slots[q:q + 1, :]).astype(f32)
         hot = jnp.where(spots == turned(ids)[:, 0:1].astype(jnp.int32), 1.0, 0.0).astype(bf16)
         span = slice(q * size, (q + 1) * size)
         part[span, :fw] = jnp.dot(hot, points[...], preferred_element_type=f32).astype(bf16)
         part[span, fw:] = jnp.dot(hot, factor[...], preferred_element_type=f32).astype(bf16)
-        for d in range(1, inner):
-            p = (place + d) % inner
-            c = remote(part.at[piece(q, p)], buf_a.at[q, d - 1], a_send.at[q, d - 1], a_recv.at[q, d - 1],
-                       layer * inner + p, col)
-            c.start()
-            step_a.append(c)
-    theirs = pl.ds(pl.multiple_of((1 - col) * half, 16), half)
-    swap = [
-        remote(points.at[theirs], other_points, x_send.at[0], x_recv.at[0], me, 1 - col),
-        remote(factor.at[theirs], other_factor, x_send.at[1], x_recv.at[1], me, 1 - col),
-    ]
-    for c in swap:
-        c.start()
+
+    def within(q, d):
+        p = (place + d) % inner
+        return remote(part.at[piece(q, p)], buf_a.at[q, d - 1], a_send.at[q, d - 1], a_recv.at[q, d - 1],
+                      layer * inner + p, col)
 
     def along(q, d):
         return remote(acc.at[q], buf_b.at[q, d - 1], b_send.at[q, d - 1], b_recv.at[q, d - 1],
@@ -132,13 +133,17 @@
         return remote(it, it, e_send.at[q, d], e_recv.at[q, d], me, 1 - col)
 
     def swap_panel(q):
-        span = pl.ds(pl.multiple_of(q * size, size), size)
+        span = slice(q * size, (q + 1) * size)
         return remote(out_ref.at[:, span], other_ref.at[:, span], f_send.at[q], f_recv.at[q], me, 1 - col)
+
+    def layer_start(q):
+        for d in range(1, inner):
+            within(q, d).start()
 
     def layer_sum(q):
         total = part[piece(q, place), :]
         for d in range(1, inner):
-            step_a[q * (inner - 1) + d - 1].wait_recv()
+            within(q, d).wait_recv()
             total = total + buf_a[q, d - 1]
         acc[q] = total
         for d in range(1, outer):
@@ -159,17 +164,28 @@
             around(q, d).wait_recv()
             across(q, d).start()
 
-    for q in range(panels):
-        layer_sum(q)
-        if q == min(2, panels - 1):
-            whole_sum(0)
-    forward(0)
-    for q in range(1, min(2, panels)):
-        whole_sum(q)
-    prow[...] = jnp.zeros_like(prow)
-    out_ref[...] = jnp.zeros_like(out_ref)
+    def arrive(q):
+        for d in range(inner):
+            across(q, d).wait_recv()
+
+    theirs = pl.ds(pl.multiple_of((1 - col) * half, 16), half)
+    swap = [
+        remote(points.at[theirs], other_points, x_send.at[0], x_recv.at[0], me, 1 - col),
+        remote(factor.at[theirs], other_factor, x_send.at[1], x_recv.at[1], me, 1 - col),
+    ]
+
+    for c in loads:
+        c.wait()
+    gather(0)
+    pl.semaphore_wait(barrier, len(peers))
+    layer_start(0)
     for c in swap:
-        c.wait_recv()
+        c.start()
+    for q in range(1, panels):
+        gather(q)
+    layer_sum(0)
+    if panels > 1:
+        layer_start(1)
 
     def norm(x, y):
         x, y = x.astype(f32), y.astype(f32)
@@ -178,12 +194,24 @@
     def dot(x, y):
         return lax.dot_general(x, y, NT, preferred_element_type=f32)
 
+    def exact(x, y):
+        return lax.dot_general(x, y, NT, precision=HIGH, preferred_element_type=f32)
+
+    for c in swap:
+        c.wait_recv()
     mine = pl.ds(pl.multiple_of(col * half, 16), half)
     own_norm = norm(points[mine, :], other_points[...])
     own_ids = lax.broadcasted_iota(jnp.int32, (half, size), 0) + (me * here + col * half)
     same = lax.broadcasted_iota(jnp.int32, (size, size), 0) == lax.broadcasted_iota(jnp.int32, (size, size), 1)
     eye = jnp.where(same, 1.0, 0.0)
 
+    whole_sum(0)
+    if panels > 1:
+        layer_sum(1)
+    if panels > 2:
+        layer_start(2)
+    forward(0)
+
     runs = gp.shape[1]
     lines = gp.shape[3]
     width = own_cols.shape[1]
@@ -213,7 +241,7 @@
 
     def gram_block(k):
         swap_panel(k).wait_recv()
-        lanes = pl.ds(pl.multiple_of(k * size, size), size)
+        lanes = slice(k * size, (k + 1) * size)
         for source, which in ((out_ref, col), (other_ref, 1 - col)):
             for i in range(half // size):
                 level = turned(weights[pl.ds(which * (half // size) + i, 1), :])[:, 0:1]
@@ -237,62 +265,96 @@
             def _():
                 gram_b(k, i).start()
 
-    def panel(q, carry):
-        for d in range(inner):
-            across(q, d).wait_recv()
-        span = pl.ds(pl.multiple_of(q * size, size), size)
-        ps, po = piv[col, span, :], piv[1 - col, span, :]
+    def span(q):
+        return slice(q * size, (q + 1) * size)
+
+    def entries(xs, xo, ys, yo, q, row_norms):
+        ts, to = piv[col, span(q), :], piv[1 - col, span(q), :]
+        cross = dot(xs, ts[:, :fw]) + dot(xo, to[:, :fw])
+        schur = dot(ys, ts[:, fw:]) + dot(yo, to[:, fw:])
+        return jnp.exp(-(row_norms + norms[q, 0:1, :] - 2.0 * cross) / feats) + schur / (3.0 * rank)
+
+    def less(value, x, y, count):
+        if count:
+            return value - dot(x[:, :count * size], y[:, :count * size])
+        return value
+
+    def head(r):
+        ps, po = piv[col, span(r), :], piv[1 - col, span(r), :]
         pnorm = norm(ps[:, :fw], po[:, :fw])
-        norms[q] = jnp.transpose(jnp.broadcast_to(pnorm, (size, size)))
-
-        def entries(xs, xo, ys, yo, ts, to, n, row_norm):
-            cross = dot(xs, ts[:, :fw]) + dot(xo, to[:, :fw])
-            schur = dot(ys, ts[:, fw:]) + dot(yo, to[:, fw:])
-            return jnp.exp(-(n + row_norm - 2.0 * cross) / feats) + schur / (3.0 * rank)
-
-        def earlier(k, carry):
-            other = pl.ds(pl.multiple_of(k * size, size), size)
-            ts, to = piv[col, other, :], piv[1 - col, other, :]
-            row_norm = norms[k][0:1, :]
-            m = entries(ps[:, :fw], po[:, :fw], ps[:, fw:], po[:, fw:], ts, to, pnorm, row_norm)
-            m = m - dot(prow[q], prow[k])
-            prow[q, :, other] = lax.dot_general(m, inv[k], NT, precision=HIGH,
-                                                preferred_element_type=f32).astype(bf16)
-            return carry
-
-        lax.fori_loop(0, q, earlier, 0)
-        row_norm = norms[q][0:1, :]
-        a[...] = (entries(ps[:, :fw], po[:, :fw], ps[:, fw:], po[:, fw:], ps, po, pnorm, row_norm)
-                  + RIDGE_LEVEL * eye - dot(prow[q], prow[q]))
-        e = inv.at[q]
-        e[...] = eye
-
-        @pl.when(q + 2 < panels)
-        def _():
-            whole_sum(q + 2)
-
-        @pl.when(q + 1 < panels)
-        def _():
-            forward(q + 1)
-
-        @pl.when(q > 1)
-        def _():
-            gram_sum(q - 2)
-
-        @pl.when(q > 0)
-        def _():
-            gram_block(q - 1)
-        ids = owners[pl.ds(q, 1), :] * here + slots[pl.ds(q, 1), :]
-        columns = (entries(points[mine, :], other_points[...], factor[mine, :], other_factor[...], ps, po,
-                           own_norm, row_norm)
-                   + jnp.where(own_ids == ids, RIDGE_LEVEL, 0.0) - dot(out_ref[...], prow[q]))
-        factor_block(size, a, e, rows, None, wide)
-        out_ref[:, span] = lax.dot_general(columns, e[...], NT, precision=HIGH,
-                                           preferred_element_type=f32).astype(bf16)
-        swap_panel(q).start()
-        return carry
-
-    lax.fori_loop(0, panels, panel, 0)
+        norms[r] = jnp.transpose(jnp.broadcast_to(pnorm, (size, size)))
+
+        def against(k):
+            return entries(ps[:, :fw], po[:, :fw], ps[:, fw:], po[:, fw:], k, pnorm)
+
+        for k in range(r):
+            m = less(against(k), prow[r], prow[k], k)
+            if k < r - 1:
+                prow[r, :, span(k)] = exact(m, inv[k]).astype(bf16)
+            else:
+                ready[...] = m
+        early[...] = less(against(r) + RIDGE_LEVEL * eye, prow[r], prow[r], max(r - 1, 0))
+
+    def begin(r):
+        if r:
+            fresh = exact(ready[...], inv[r - 1]).astype(bf16)
+            prow[r, :, span(r - 1)] = fresh
+            a[...] = early[...] - dot(fresh, fresh)
+        else:
+            a[...] = early[...]
+        inv[r] = eye
+
+    def solve(r):
+        out_ref[:, span(r)] = exact(columns[...], inv[r]).astype(bf16)
+
+    def fill(r):
+        ids = owners[r:r + 1, :] * here + slots[r:r + 1, :]
+        value = entries(points[mine, :], other_points[...], factor[mine, :], other_factor[...], r, own_norm)
+        value = value + jnp.where(own_ids == ids, RIDGE_LEVEL, 0.0)
+        columns[...] = less(value, out_ref, prow[r], r)
+
+    arrive(0)
+    head(0)
+    for q in range(panels):
+        def first_hook():
+            if q == 0 and panels > 1:
+                whole_sum(1)
+                if panels > 2:
+                    layer_sum(2)
+                if panels > 3:
+                    layer_start(3)
+            if q > 0:
+                swap_panel(q - 1).start()
+            if q > 0 and q + 1 < panels:
+                forward(q + 1)
+
+        def second_hook():
+            if q == 0 and panels > 1:
+                forward(1)
+            if q + 2 < panels:
+                whole_sum(q + 2)
+            if q + 3 < panels:
+                layer_sum(q + 3)
+            if q > 0:
+                gram_block(q - 1)
+            if q > 1:
+                gram_sum(q - 2)
+            if q > 0 and q + 1 < panels:
+                arrive(q + 1)
+                head(q + 1)
+
+        def third_hook():
+            if q == 0 and panels > 1:
+                arrive(1)
+                head(1)
+
+        begin(q)
+        if q:
+            solve(q - 1)
+        fill(q)
+        factor_block(size, a, inv.at[q], rows, wide, {4 * BLOCK: first_hook, 10 * BLOCK: second_hook, 14 * BLOCK: third_hook})
+    solve(panels - 1)
+    swap_panel(panels - 1).start()
     if panels > 1:
         gram_sum(panels - 2)
     gram_block(panels - 1)
@@ -325,11 +387,12 @@
         new_a(d).wait_send()
     for d in range(1, outer):
         new_b(d).wait_send()
-    for c in step_a + swap:
+    for c in swap:
         c.wait_send()
     for q in range(panels):
         swap_panel(q).wait_send()
         for d in range(1, inner):
+            within(q, d).wait_send()
             gram_a(q, d).wait_send()
         for i in range(runs):
             @pl.when(layer != q * runs + i)
@@ -341,6 +404,14 @@
             around(q, d).wait_send()
         for d in range(inner):
             across(q, d).wait_send()
+
+
+def write_kernel(a, b, c, x, y, z, sems):
+    copies = [pltpu.make_async_copy(s, d, sems.at[i]) for i, (s, d) in enumerate(((a, x), (b, y), (c, z)))]
+    for c in copies:
+        c.start()
+    for c in copies:
+        c.wait()
 
 
 def body(points, factor, weights, pivot_slots, pivot_owners):
@@ -354,6 +425,7 @@
     half = here // 2
     bf16, f32 = jnp.bfloat16, jnp.float32
     vm = pl.BlockSpec(memory_space=VMEM)
+    hbm = pl.BlockSpec(memory_space=pl.ANY)
     sem = lambda *n: pltpu.SemaphoreType.DMA(n)
     limit = 60 * 1024 * 1024
 
@@ -363,14 +435,12 @@
     runs = layers // panels
     share = count // 2
     scale = size / math.sqrt(here * rows)
-    return pl.pallas_call(
+    outs = pl.pallas_call(
         functools.partial(panel_kernel, split, layers, scale),
         out_shape=(
-            jax.ShapeDtypeStruct((here, share), bf16),
-            jax.ShapeDtypeStruct((chunk, rank), f32),
-            jax.ShapeDtypeStruct((chunk, share), f32),
+            pltpu.VMEM((here, share), bf16), pltpu.VMEM((chunk, rank), f32), pltpu.VMEM((chunk, share), f32),
         ),
-        in_specs=[vm] * 5, out_specs=(vm,) * 3, name="panels",
+        in_specs=[vm, vm, hbm, hbm, vm], out_specs=(vm,) * 3, name="panels",
         scratch_shapes=[
             VMEM((half, count), bf16), VMEM((half, count), bf16), VMEM((count, here), bf16),
             VMEM((panels, runs, split, chunk, rank), bf16),
@@ -383,6 +453,7 @@
             VMEM((layers - 1, chunk, share), bf16),
             sem(panels, split - 1), sem(panels, split - 1), sem(panels, runs), sem(layers),
             sem(split - 1), sem(split - 1), sem(layers - 1), sem(layers - 1),
+            VMEM((here, fw), bf16), VMEM((here, rank), bf16), sem(2),
             VMEM((count, width), bf16), VMEM((2, count, width), bf16),
             VMEM((half, fw), bf16), VMEM((half, rank), bf16),
             VMEM((panels, split - 1, piece, width), bf16),
@@ -390,6 +461,7 @@
             VMEM((panels, piece, width), bf16),
             VMEM((panels, size, count), bf16),
             VMEM((panels, size, size), f32), VMEM((panels, size, size), f32), VMEM((size, size), f32),
+            VMEM((size, size), f32), VMEM((size, size), f32), VMEM((half, size), f32),
             VMEM((2 * BLOCK, size), f32), VMEM((2 * BLOCK, BLOCK, size), f32),
             sem(panels, split - 1), sem(panels, split - 1), sem(panels, layers - 1), sem(panels, layers - 1),
             sem(panels), sem(panels), sem(panels, split - 1), sem(panels, split - 1),
@@ -397,6 +469,16 @@
         ],
         compiler_params=pltpu.CompilerParams(collective_id=0, has_side_effects=True, vmem_limit_bytes=limit),
     )(pivot_slots, pivot_owners, points, factor, weights.reshape(here // size, size))
+    return pl.pallas_call(
+        write_kernel,
+        out_shape=(
+            jax.ShapeDtypeStruct((here, share), bf16),
+            jax.ShapeDtypeStruct((chunk, rank), f32),
+            jax.ShapeDtypeStruct((chunk, share), f32),
+        ),
+        in_specs=[vm] * 3, out_specs=(hbm,) * 3, name="write",
+        scratch_shapes=[sem(3)],
+    )(*[pltpu.with_memory_space_constraint(v, pltpu.VMEM) for v in outs])
 
 
 def solution(mesh):

time: 82.1 us -> 69 us (0.84)
  Pallas kernels: 78 us -> 68 us
  local copies, waits for them, and re-layouts: 3.25 us -> 0 us
    pallas_call x1, Pallas kernels: 78 us -> 67.1 us  [body(): pl.pallas_call(functools.partial(panel_kernel, split, layers, scale), out...]
    unnamed x7 -> x0, local copies, waits for them, and re-layouts: 3.25 us -> none
    pallas_call x0 -> x1, Pallas kernels: none -> 0.88 us  [body(): pl.pallas_call(write_kernel, out_shape=(jax.ShapeDtypeStruct((here, share...]
where the time goes in v1:
time: 69 us; the launch traced here: 68.8 us
  Pallas kernels  68 us (99%)
  between operations  0.8 us (1%)
    pallas_call x1, Pallas kernels, body(): pl.pallas_call(functools.partial(panel_kernel, split, layers, scale), out...  67.1 us

profile of v1, /device:TPU:0, one launch (start us, length us, event | category | flops | bytes accessed | tf_op | source)
XLA Modules:
  0.0 68.8 jit_solution(11239621896548503898)
XLA Ops:
  0.6 67.1 %panels.1 = (bf16[1280,256]{1,0:T(8,128)(2,1)S(1)}, f32[32,512]{1,0:T(8,128)S(1)}, f32[32,256]{1,0:T(8,128)S(1)}) custom-call(s32[4,128]{1,0:T(4,128)} %slots.1, s32[4,128]{1,0:T(4,128)} %owners.1, bf16[1280,256]{1,0:T(8,128)(2,1)} %points_in.1, bf16[1280,512]{1,0:T(8,128)(2,1)} %factor_in.1, f32[10,128]{1,0:T(8,128)} %bitcast.1), custom_call_target="tpu_custom_call" | custom-call | tf_op jit(solution)/shard_map/panels/pallas_call | solution.py:438
  67.7 0.9 %write.1 = (bf16[1280,256]{1,0:T(8,128)(2,1)}, f32[32,512]{1,0:T(8,128)}, f32[32,256]{1,0:T(8,128)}) custom-call(bf16[1280,256]{1,0:T(8,128)(2,1)S(1)} %get-tuple-element.6.a, f32[32,512]{1,0:T(8,128)S(1)} %get-tuple-element.7.b, f32[32,256]{1,0:T(8,128)S(1)} %get-tuple-element.8.c), custom_call_target="tpu_custom_call" | custom-call | tf_op jit(solution)/shard_map/write/pallas_call | solution.py:472

commit v2 on v1

--- a/solution.py
+++ b/solution.py
@@ -10,6 +10,7 @@
 
 RIDGE_LEVEL = 1.0
 BLOCK = 8
+HOOKS = (4, 8, 12, 14)
 VMEM = pltpu.VMEM
 HIGH = lax.Precision.HIGHEST
 NT = (((1,), (1,)), ((), ()))
@@ -31,52 +32,97 @@
     return peers
 
 
-def factor_block(size, a, e, rows, wide, hooks):
-    for first in range(0, size, BLOCK):
+def pivot_chain(d):
+    scales = []
+    for k in range(0, BLOCK, 2):
+        first = lax.rsqrt(d[k, k])
+        both = lax.rsqrt(d[k, k] * d[k + 1, k + 1] - d[k + 1, k] * d[k + 1, k])
+        scales += [first, both * (d[k, k] * first)]
+        step = both * first
+        for i in range(k + 2, BLOCK):
+            d[i, k + 1] = (d[k, k] * d[i, k + 1] - d[i, k] * d[k + 1, k]) * step
+        for i in range(k + 1, BLOCK):
+            d[i, k] = d[i, k] * first
+        for i in range(k + 2, BLOCK):
+            for m in range(k + 2, i + 1):
+                d[i, m] = d[i, m] - d[i, k] * d[m, k] - d[i, k + 1] * d[m, k + 1]
+    return scales
+
+
+def solve_rows(d, scales, z):
+    for k in range(BLOCK):
+        z[k] = z[k] * scales[k]
+        for i in range(k + 1, BLOCK):
+            z[i] = z[i] - d[i, k] * z[k]
+    return z
+
+
+def factor_block(size, x, rows, wide, hooks):
+    deep = 2 * BLOCK
+    lane = lax.broadcasted_iota(jnp.int32, (BLOCK, size), 1)
+    line = lax.broadcasted_iota(jnp.int32, (BLOCK, size), 0)
+
+    def full(ref, i):
+        return jnp.broadcast_to(ref[i:i + 1, :], (BLOCK, size))
+
+    for first in range(0, size, deep):
         if first in hooks:
             hooks[first]()
-        span = slice(first, first + BLOCK)
-        strip = a[span, :]
+        turn = first // deep % 2
+        base, at = 3 * BLOCK * turn, deep * turn
+        middle, after = first + BLOCK, first + deep
+        inside = (lane >= first) & (lane < after)
+        top = x[first:middle, :]
+        low = x[middle:after, :]
         for k in range(BLOCK):
-            wide[first // BLOCK % 2 * BLOCK + k] = jnp.broadcast_to(strip[:, first + k:first + k + 1], (BLOCK, size))
-        d = {(i, k): wide[first // BLOCK % 2 * BLOCK + k, i:i + 1, :] for i in range(BLOCK) for k in range(i + 1)}
-        r = [a[first + i:first + i + 1, :] for i in range(BLOCK)]
-        s = [e[first + i:first + i + 1, :] for i in range(BLOCK)]
+            for slot, part, spot in ((0, top, first + k), (1, low, first + k), (2, low, middle + k)):
+                wide[base + slot * BLOCK + k] = jnp.broadcast_to(part[:, spot:spot + 1], (BLOCK, size))
+        d = {(i, k): full(wide.at[base + k], i) for i in range(BLOCK) for k in range(i + 1)}
+        scales = pivot_chain(d)
+        left = []
         for k in range(BLOCK):
-            scale = lax.rsqrt(d[k, k])
-            r[k] = r[k] * scale
-            s[k] = s[k] * scale
-            for i in range(k + 1, BLOCK):
-                d[i, k] = d[i, k] * scale
-            for i in range(k + 1, BLOCK):
-                r[i] = r[i] - d[i, k] * r[k]
-                s[i] = s[i] - d[i, k] * s[k]
-                for m in range(k + 1, i + 1):
-                    d[i, m] = d[i, m] - d[i, k] * d[m, k]
-        base = BLOCK * (first // BLOCK % 2)
+            w = wide[base + BLOCK + k]
+            for m in range(k):
+                w = w - d[k, m] * left[m]
+            left.append(w * scales[k])
+            wide[base + BLOCK + k] = left[k]
+        z = [jnp.where(inside, jnp.where(lane == first + i, 1.0, 0.0), full(x, first + i)) for i in range(BLOCK)]
+        z = solve_rows(d, scales, z)
+        under = jnp.where(inside, jnp.where(lane == middle + line, 1.0, 0.0), low)
         for k in range(BLOCK):
-            rows[base + k:base + k + 1, :] = r[k]
-            e[first + k:first + k + 1, :] = s[k]
-        after = first + BLOCK
+            under = under - left[k] * z[k]
+            rows[at + k:at + k + 1, :] = z[k][0:1, :]
+        x[middle:after, :] = under
+        for m in range(BLOCK):
+            v = wide[base + 2 * BLOCK + m]
+            for k in range(BLOCK):
+                v = v - left[k] * full(wide.at[base + BLOCK + k], m)
+            wide[base + 2 * BLOCK + m] = v
+        d = {(i, k): full(wide.at[base + 2 * BLOCK + k], i) for i in range(BLOCK) for k in range(i + 1)}
+        scales = pivot_chain(d)
+        z = solve_rows(d, scales, [full(x, middle + i) for i in range(BLOCK)])
+        for k in range(BLOCK):
+            rows[at + BLOCK + k:at + BLOCK + k + 1, :] = z[k][0:1, :]
+        done = rows[at:at + deep, :]
+        x[first:after, :] = jnp.where(lax.broadcasted_iota(jnp.int32, (deep, size), 1) < after, done, 0.0)
         if after < size:
-            upper = jnp.transpose(rows[base:base + BLOCK, :])
-            for low, high in ((after, after + BLOCK), (after + BLOCK, size)):
-                if low < high:
-                    rest_a = a[low:high, :]
-                    rest_e = e[low:high, :]
-                    for k in range(BLOCK):
-                        column = upper[low:high, k:k + 1]
-                        rest_a = rest_a - column * rows[base + k:base + k + 1, :]
-                        rest_e = rest_e - column * e[first + k:first + k + 1, :]
-                    a[low:high, :] = rest_a
-                    e[low:high, :] = rest_e
+            upper = jnp.transpose(done)
+            for start, stop in ((after, after + deep), (after + deep, size)):
+                if start < stop:
+                    spots = lax.broadcasted_iota(jnp.int32, (stop - start, size), 1)
+                    rest = jnp.where((spots >= first) & (spots < after), 0.0, x[start:stop, :])
+                    for k in range(deep):
+                        rest = rest - upper[start:stop, k:k + 1] * rows[at + k:at + k + 1, :]
+                    x[start:stop, :] = rest
 
 
 def panel_kernel(inner, outer, scale_by, slots, owners, points_in, factor_in, weights, own_cols, gram_old, gram_new,
                  out_ref, other_ref, level_t, gp, ga, gacc, gmid, gb, nw, na, nacc, nmid, nb,
+                 cw, ca, cacc, cmid, cb,
                  ga_send, ga_recv, gb_send, gb_recv, na_send, na_recv, nb_send, nb_recv,
+                 ca_send, ca_recv, cb_send, cb_recv,
                  points, factor, load, part, piv, other_points, other_factor, buf_a, buf_b, acc,
-                 prow, inv, norms, a, early, ready, columns, rows, wide,
+                 prow, inv, norms, early, ready, columns, rows, wide,
                  a_send, a_recv, b_send, b_recv, f_send, f_recv,
                  d_send, d_recv, e_send, e_recv, x_send, x_recv):
     me = lax.axis_index("rows")
@@ -183,9 +229,13 @@
         c.start()
     for q in range(1, panels):
         gather(q)
+        if q == 1:
+            layer_start(1)
     layer_sum(0)
     if panels > 1:
-        layer_start(1)
+        layer_sum(1)
+    if panels > 2:
+        layer_start(2)
 
     def norm(x, y):
         x, y = x.astype(f32), y.astype(f32)
@@ -205,17 +255,18 @@
     same = lax.broadcasted_iota(jnp.int32, (size, size), 0) == lax.broadcasted_iota(jnp.int32, (size, size), 1)
     eye = jnp.where(same, 1.0, 0.0)
 
+    if panels > 2:
+        layer_sum(2)
     whole_sum(0)
+    if panels > 3:
+        layer_start(3)
+    forward(0)
     if panels > 1:
-        layer_sum(1)
-    if panels > 2:
-        layer_start(2)
-    forward(0)
+        whole_sum(1)
 
     runs = gp.shape[1]
     lines = gp.shape[3]
     width = own_cols.shape[1]
-    wide_lanes = pl.ds(pl.multiple_of(col * width, 128), width)
 
     def gram_a(k, d):
         p = (place + d) % inner
@@ -231,25 +282,86 @@
         return remote(gmid.at[0, 0], gb.at[d - 1], gb_send.at[0, 0], gb_recv.at[d - 1],
                       ((layer + d) % outer) * inner + place, col)
 
-    def new_a(d):
+    cut = outer - runs
+    count = panels * size
+
+    def half_rows(which):
+        return pl.ds(pl.multiple_of(which * half, 16), half)
+
+    def slot_of(z):
+        return (layer - z + 2 * outer - 1) % outer
+
+    def new_a(late, d):
         p = (place + d) % inner
-        return remote(nw.at[:, p], na.at[d - 1], na_send.at[d - 1], na_recv.at[d - 1], layer * inner + p, col)
-
-    def new_b(d):
-        z = (layer + d) % outer
-        return remote(nmid.at[z], nb.at[d - 1], nb_send.at[d - 1], nb_recv.at[d - 1], z * inner + place, col)
+        rows_of = slice(cut, outer) if late else slice(0, cut)
+        return remote(nw.at[rows_of, p], na.at[d - 1, rows_of], na_send.at[late, d - 1], na_recv.at[late, d - 1],
+                      layer * inner + p, col)
+
+    def new_b(z):
+        return remote(nmid.at[z], nb.at[slot_of(z)], nb_send.at[z], nb_recv.at[slot_of(z)], z * inner + place, col)
+
+    def new_got(d):
+        return remote(nmid.at[0], nb.at[d - 1], nb_send.at[0], nb_recv.at[d - 1],
+                      ((layer + d) % outer) * inner + place, col)
+
+    def side_a(d):
+        p = (place + d) % inner
+        return remote(cw.at[:, p], ca.at[d - 1], ca_send.at[d - 1], ca_recv.at[d - 1], layer * inner + p, col)
+
+    def side_b(z):
+        return remote(cmid.at[z], cb.at[slot_of(z)], cb_send.at[z], cb_recv.at[slot_of(z)], z * inner + place, col)
+
+    def side_got(d):
+        return remote(cmid.at[0], cb.at[d - 1], cb_send.at[0], cb_recv.at[d - 1],
+                      ((layer + d) % outer) * inner + place, col)
+
+    def new_early():
+        for source, which in ((out_ref, col), (other_ref, 1 - col)):
+            own_cols[half_rows(which), :width - size] = source[:, pl.ds(pl.multiple_of(col * width, 128), width - size)]
+
+        @pl.when(col == 0)
+        def _():
+            for source, which in ((out_ref, col), (other_ref, 1 - col)):
+                own_cols[half_rows(which), width - size:] = source[:, width - size:width]
+
+        @pl.when(col == 1)
+        def _():
+            own_cols[:, width - size:] = jnp.zeros((here, size), bf16)
+
+        block = jnp.dot(level_t[:count - size, :], own_cols[...], preferred_element_type=f32) * scale_by
+        nw[:cut] = block.reshape(cut, inner, lines, width).astype(bf16)
+
+    def new_sum(late):
+        rows_of = slice(cut, outer) if late else slice(0, cut)
+        total = nw[rows_of, place].astype(f32)
+        for d in range(1, inner):
+            new_a(late, d).wait_recv()
+            total = total + na[d - 1, rows_of].astype(f32)
+        nacc[rows_of] = total
+        nmid[rows_of] = total.astype(bf16)
+        for z in range(outer)[rows_of]:
+            @pl.when(layer != z)
+            def _():
+                new_b(z).start()
 
     def gram_block(k):
-        swap_panel(k).wait_recv()
         lanes = slice(k * size, (k + 1) * size)
-        for source, which in ((out_ref, col), (other_ref, 1 - col)):
+
+        def part_of(source, which):
             for i in range(half // size):
                 level = turned(weights[pl.ds(which * (half // size) + i, 1), :])[:, 0:1]
                 block = source[i * size:(i + 1) * size, lanes].astype(f32) * level
                 first = pl.multiple_of(which * half + i * size, size)
                 level_t[lanes, pl.ds(first, size)] = jnp.transpose(block).astype(bf16)
-        block = jnp.dot(level_t[lanes, :], factor[...], preferred_element_type=f32) * scale_by
+            spots = pl.ds(pl.multiple_of(which * half, size), half)
+            return jnp.dot(level_t[lanes, spots], factor[half_rows(which), :], preferred_element_type=f32)
+
+        block = part_of(out_ref, col)
+        swap_panel(k).wait_recv()
+        block = (block + part_of(other_ref, 1 - col)) * scale_by
         gp[k] = block.reshape(runs, inner, lines, factor.shape[1]).astype(bf16)
+
+    def gram_send(k):
         for d in range(1, inner):
             gram_a(k, d).start()
 
@@ -299,10 +411,9 @@
         if r:
             fresh = exact(ready[...], inv[r - 1]).astype(bf16)
             prow[r, :, span(r - 1)] = fresh
-            a[...] = early[...] - dot(fresh, fresh)
+            inv[r] = early[...] - dot(fresh, fresh)
         else:
-            a[...] = early[...]
-        inv[r] = eye
+            inv[r] = early[...]
 
     def solve(r):
         out_ref[:, span(r)] = exact(columns[...], inv[r]).astype(bf16)
@@ -316,63 +427,83 @@
     arrive(0)
     head(0)
     for q in range(panels):
-        def first_hook():
-            if q == 0 and panels > 1:
-                whole_sum(1)
-                if panels > 2:
-                    layer_sum(2)
-                if panels > 3:
-                    layer_start(3)
+        def early_hook():
             if q > 0:
                 swap_panel(q - 1).start()
-            if q > 0 and q + 1 < panels:
+
+        def middle_hook():
+            if q == 0 and panels > 3:
+                layer_sum(3)
+            if q > 0:
+                gram_block(q - 1)
+            if q == panels - 1:
+                new_early()
+
+        def late_hook():
+            if q > 0:
+                gram_send(q - 1)
+            if q == panels - 1:
+                for d in range(1, inner):
+                    new_a(0, d).start()
+            if q + 1 < panels:
                 forward(q + 1)
 
-        def second_hook():
-            if q == 0 and panels > 1:
-                forward(1)
+        def last_hook():
             if q + 2 < panels:
                 whole_sum(q + 2)
-            if q + 3 < panels:
-                layer_sum(q + 3)
-            if q > 0:
-                gram_block(q - 1)
             if q > 1:
                 gram_sum(q - 2)
-            if q > 0 and q + 1 < panels:
-                arrive(q + 1)
-                head(q + 1)
-
-        def third_hook():
-            if q == 0 and panels > 1:
-                arrive(1)
-                head(1)
 
         begin(q)
         if q:
             solve(q - 1)
         fill(q)
-        factor_block(size, a, inv.at[q], rows, wide, {4 * BLOCK: first_hook, 10 * BLOCK: second_hook, 14 * BLOCK: third_hook})
+        factor_block(size, inv.at[q], rows, wide, {
+            HOOKS[0] * BLOCK: early_hook, HOOKS[1] * BLOCK: middle_hook,
+            HOOKS[2] * BLOCK: late_hook, HOOKS[3] * BLOCK: last_hook})
+        if q + 1 < panels:
+            arrive(q + 1)
+            head(q + 1)
     solve(panels - 1)
     swap_panel(panels - 1).start()
-    if panels > 1:
-        gram_sum(panels - 2)
     gram_block(panels - 1)
-    for source, which in ((out_ref, col), (other_ref, 1 - col)):
-        own_cols[pl.ds(pl.multiple_of(which * half, 16), half), :] = source[:, wide_lanes]
-    block = jnp.dot(level_t[...], own_cols[...], preferred_element_type=f32) * scale_by
-    nw[...] = block.reshape(outer, inner, lines, width).astype(bf16)
+    gram_send(panels - 1)
+
+    @pl.when(col == 1)
+    def _():
+        for source, which in ((out_ref, col), (other_ref, 1 - col)):
+            own_cols[half_rows(which), width - size:] = source[:, count - size:]
+
+    block = jnp.dot(level_t[count - size:, :], own_cols[...], preferred_element_type=f32) * scale_by
+    nw[cut:] = block.reshape(outer - cut, inner, lines, width).astype(bf16)
     for d in range(1, inner):
-        new_a(d).start()
+        new_a(1, d).start()
+
+    @pl.when(col == 1)
+    def _():
+        block = jnp.dot(level_t[:count - size, :], own_cols[:, width - size:], preferred_element_type=f32) * scale_by
+        cw[...] = block.reshape(cut, inner, lines, size).astype(bf16)
+        for d in range(1, inner):
+            side_a(d).start()
+
+    gram_sum(panels - 2)
+    new_sum(0)
     gram_sum(panels - 1)
-    total = nw[:, place].astype(f32)
-    for d in range(1, inner):
-        new_a(d).wait_recv()
-        total = total + na[d - 1].astype(f32)
-    nacc[...] = total
-    nmid[...] = total.astype(bf16)
-    for d in range(1, outer):
-        new_b(d).start()
+    new_sum(1)
+
+    @pl.when(col == 1)
+    def _():
+        total = cw[:, place].astype(f32)
+        for d in range(1, inner):
+            side_a(d).wait_recv()
+            total = total + ca[d - 1].astype(f32)
+        cacc[...] = total
+        cmid[...] = total.astype(bf16)
+        for z in range(cut):
+            @pl.when(layer != z)
+            def _():
+                side_b(z).start()
+
     total = gacc[layer // runs, layer % runs]
     for d in range(1, outer):
         gram_got(d).wait_recv()
@@ -380,13 +511,35 @@
     gram_old[...] = total
     total = nacc[layer]
     for d in range(1, outer):
-        new_b(d).wait_recv()
+        new_got(d).wait_recv()
         total = total + nb[d - 1].astype(f32)
     gram_new[...] = total
+
+    @pl.when((col == 1) & (layer < cut))
+    def _():
+        total = gram_new[:, width - size:] + cacc[jnp.minimum(layer, cut - 1)]
+        for d in range(1, outer):
+            side_got(d).wait_recv()
+            total = total + cb[d - 1].astype(f32)
+        gram_new[:, width - size:] = total
+
     for d in range(1, inner):
-        new_a(d).wait_send()
-    for d in range(1, outer):
-        new_b(d).wait_send()
+        new_a(0, d).wait_send()
+        new_a(1, d).wait_send()
+    for z in range(outer):
+        @pl.when(layer != z)
+        def _():
+            new_b(z).wait_send()
+
+    @pl.when(col == 1)
+    def _():
+        for d in range(1, inner):
+            side_a(d).wait_send()
+        for z in range(cut):
+            @pl.when(layer != z)
+            def _():
+                side_b(z).wait_send()
+
     for c in swap:
         c.wait_send()
     for q in range(panels):
@@ -433,6 +586,7 @@
     layers = rows // split
     piece = size // split
     runs = layers // panels
+    cut = layers - runs
     share = count // 2
     scale = size / math.sqrt(here * rows)
     outs = pl.pallas_call(
@@ -451,8 +605,11 @@
             VMEM((split - 1, layers, chunk, share), bf16),
             VMEM((layers, chunk, share), f32), VMEM((layers, chunk, share), bf16),
             VMEM((layers - 1, chunk, share), bf16),
+            VMEM((cut, split, chunk, size), bf16), VMEM((split - 1, cut, chunk, size), bf16),
+            VMEM((cut, chunk, size), f32), VMEM((cut, chunk, size), bf16), VMEM((layers - 1, chunk, size), bf16),
             sem(panels, split - 1), sem(panels, split - 1), sem(panels, runs), sem(layers),
-            sem(split - 1), sem(split - 1), sem(layers - 1), sem(layers - 1),
+            sem(2, split - 1), sem(2, split - 1), sem(layers), sem(layers - 1),
+            sem(split - 1), sem(split - 1), sem(cut), sem(layers - 1),
             VMEM((here, fw), bf16), VMEM((here, rank), bf16), sem(2),
             VMEM((count, width), bf16), VMEM((2, count, width), bf16),
             VMEM((half, fw), bf16), VMEM((half, rank), bf16),
@@ -460,9 +617,9 @@
             VMEM((panels, layers - 1, piece, width), bf16),
             VMEM((panels, piece, width), bf16),
             VMEM((panels, size, count), bf16),
-            VMEM((panels, size, size), f32), VMEM((panels, size, size), f32), VMEM((size, size), f32),
+            VMEM((panels, size, size), f32), VMEM((panels, size, size), f32),
             VMEM((size, size), f32), VMEM((size, size), f32), VMEM((half, size), f32),
-            VMEM((2 * BLOCK, size), f32), VMEM((2 * BLOCK, BLOCK, size), f32),
+            VMEM((4 * BLOCK, size), f32), VMEM((6 * BLOCK, BLOCK, size), f32),
             sem(panels, split - 1), sem(panels, split - 1), sem(panels, layers - 1), sem(panels, layers - 1),
             sem(panels), sem(panels), sem(panels, split - 1), sem(panels, split - 1),
             sem(panels, split), sem(panels, split), sem(2), sem(2),

time: 69 us -> 62.3 us (0.903)
  the two profiles are of different devices: /device:TPU:0 before, /device:TPU:1 now
where the time goes in v2:
time: 62.3 us; the launch traced here: 62.1 us
  Pallas kernels  61.3 us (98%)
  between operations  0.8 us (1%)
    pallas_call x1, Pallas kernels, body(): pl.pallas_call(functools.partial(panel_kernel, split, layers, scale), out...  60.4 us

profile of v2, /device:TPU:1, one launch (start us, length us, event | category | flops | bytes accessed | tf_op | source)
XLA Modules:
  0.0 62.1 jit_solution(18036105963253528585)
XLA Ops:
  0.6 60.4 %panels.1 = (bf16[1280,256]{1,0:T(8,128)(2,1)S(1)}, f32[32,512]{1,0:T(8,128)S(1)}, f32[32,256]{1,0:T(8,128)S(1)}) custom-call(s32[4,128]{1,0:T(4,128)} %slots.1, s32[4,128]{1,0:T(4,128)} %owners.1, bf16[1280,256]{1,0:T(8,128)(2,1)} %points_in.1, bf16[1280,512]{1,0:T(8,128)(2,1)} %factor_in.1, f32[10,128]{1,0:T(8,128)} %bitcast.1), custom_call_target="tpu_custom_call" | custom-call | tf_op jit(solution)/shard_map/panels/pallas_call | solution.py:592
  61.0 0.9 %write.1 = (bf16[1280,256]{1,0:T(8,128)(2,1)}, f32[32,512]{1,0:T(8,128)}, f32[32,256]{1,0:T(8,128)}) custom-call(bf16[1280,256]{1,0:T(8,128)(2,1)S(1)} %get-tuple-element.6.a, f32[32,512]{1,0:T(8,128)S(1)} %get-tuple-element.7.b, f32[32,256]{1,0:T(8,128)S(1)} %get-tuple-element.8.c), custom_call_target="tpu_custom_call" | custom-call | tf_op jit(solution)/shard_map/write/pallas_call | solution.py:629

commit v3 on v2

--- a/solution.py
+++ b/solution.py
@@ -10,7 +10,7 @@
 
 RIDGE_LEVEL = 1.0
 BLOCK = 8
-HOOKS = (4, 8, 12, 14)
+HOOKS = (4, 8, 10, 12, 14)
 VMEM = pltpu.VMEM
 HIGH = lax.Precision.HIGHEST
 NT = (((1,), (1,)), ((), ()))
@@ -121,7 +121,7 @@
                  cw, ca, cacc, cmid, cb,
                  ga_send, ga_recv, gb_send, gb_recv, na_send, na_recv, nb_send, nb_recv,
                  ca_send, ca_recv, cb_send, cb_recv,
-                 points, factor, load, part, piv, other_points, other_factor, buf_a, buf_b, acc,
+                 points, factor, load, part, piv, other_points, other_factor, buf_a, buf_b, acc, mid,
                  prow, inv, norms, early, ready, columns, rows, wide,
                  a_send, a_recv, b_send, b_recv, f_send, f_recv,
                  d_send, d_recv, e_send, e_recv, x_send, x_recv):
@@ -186,20 +186,46 @@
         for d in range(1, inner):
             within(q, d).start()
 
+    steps = (outer - 1).bit_length()
+    paired = outer == 1 << steps
+
+    def twice(q, j):
+        away = layer + (1 << j) - (2 << j) * (layer // (1 << j) % 2)
+        source = mid.at[q, j - 1] if j else acc.at[q]
+        return remote(source, buf_b.at[q, j], b_send.at[q, j], b_recv.at[q, j], away * inner + place, col)
+
+    def sends_b(q):
+        if q and paired:
+            return [twice(q, j) for j in range(steps)]
+        return [along(q, d) for d in range(1, outer)]
+
     def layer_sum(q):
         total = part[piece(q, place), :]
         for d in range(1, inner):
             within(q, d).wait_recv()
             total = total + buf_a[q, d - 1]
         acc[q] = total
-        for d in range(1, outer):
-            along(q, d).start()
+        for c in sends_b(q)[:1 if q and paired else outer]:
+            c.start()
+
+    def between(q):
+        if paired:
+            total = acc[q]
+            for j in range(1, steps):
+                twice(q, j - 1).wait_recv()
+                total = total + buf_b[q, j - 1]
+                mid[q, j - 1] = total
+                twice(q, j).start()
 
     def whole_sum(q):
-        total = acc[q]
-        for d in range(1, outer):
-            along(q, d).wait_recv()
-            total = total + buf_b[q, d - 1]
+        if q and paired:
+            twice(q, steps - 1).wait_recv()
+            total = (mid[q, steps - 2] if steps > 1 else acc[q]) + buf_b[q, steps - 1]
+        else:
+            total = acc[q]
+            for d in range(1, outer):
+                along(q, d).wait_recv()
+                total = total + buf_b[q, d - 1]
         piv[col, piece(q, place)] = total
         for d in range(1, inner):
             around(q, d).start()
@@ -229,13 +255,11 @@
         c.start()
     for q in range(1, panels):
         gather(q)
-        if q == 1:
-            layer_start(1)
-    layer_sum(0)
-    if panels > 1:
-        layer_sum(1)
-    if panels > 2:
-        layer_start(2)
+        layer_start(q)
+    for q in range(panels):
+        layer_sum(q)
+        if q == 2:
+            between(1)
 
     def norm(x, y):
         x, y = x.astype(f32), y.astype(f32)
@@ -255,14 +279,11 @@
     same = lax.broadcasted_iota(jnp.int32, (size, size), 0) == lax.broadcasted_iota(jnp.int32, (size, size), 1)
     eye = jnp.where(same, 1.0, 0.0)
 
-    if panels > 2:
-        layer_sum(2)
     whole_sum(0)
-    if panels > 3:
-        layer_start(3)
+    for q in range(2, panels):
+        between(q)
     forward(0)
-    if panels > 1:
-        whole_sum(1)
+    whole_sum(1)
 
     runs = gp.shape[1]
     lines = gp.shape[3]
@@ -427,30 +448,41 @@
     arrive(0)
     head(0)
     for q in range(panels):
-        def early_hook():
+        def hook_a():
             if q > 0:
                 swap_panel(q - 1).start()
-
-        def middle_hook():
-            if q == 0 and panels > 3:
-                layer_sum(3)
+            if q == 0:
+                whole_sum(2)
+            if q == 1:
+                forward(2)
+
+        def hook_b():
             if q > 0:
                 gram_block(q - 1)
             if q == panels - 1:
                 new_early()
 
-        def late_hook():
+        def hook_c():
+            if q == 0:
+                forward(1)
+                whole_sum(3)
+            elif q + 1 < panels:
+                arrive(q + 1)
+                head(q + 1)
+
+        def hook_d():
             if q > 0:
                 gram_send(q - 1)
             if q == panels - 1:
                 for d in range(1, inner):
                     new_a(0, d).start()
-            if q + 1 < panels:
-                forward(q + 1)
-
-        def last_hook():
-            if q + 2 < panels:
-                whole_sum(q + 2)
+            if q == 1:
+                forward(3)
+
+        def hook_e():
+            if q == 0:
+                arrive(1)
+                head(1)
             if q > 1:
                 gram_sum(q - 2)
 
@@ -458,12 +490,8 @@
         if q:
             solve(q - 1)
         fill(q)
-        factor_block(size, inv.at[q], rows, wide, {
-            HOOKS[0] * BLOCK: early_hook, HOOKS[1] * BLOCK: middle_hook,
-            HOOKS[2] * BLOCK: late_hook, HOOKS[3] * BLOCK: last_hook})
-        if q + 1 < panels:
-            arrive(q + 1)
-            head(q + 1)
+        hooks = dict(zip((at * BLOCK for at in HOOKS), (hook_a, hook_b, hook_c, hook_d, hook_e)))
+        factor_block(size, inv.at[q], rows, wide, hooks)
     solve(panels - 1)
     swap_panel(panels - 1).start()
     gram_block(panels - 1)
@@ -551,8 +579,8 @@
             @pl.when(layer != q * runs + i)
             def _():
                 gram_b(q, i).wait_send()
-        for d in range(1, outer):
-            along(q, d).wait_send()
+        for c in sends_b(q):
+            c.wait_send()
         for d in range(1, inner):
             around(q, d).wait_send()
         for d in range(inner):
@@ -615,7 +643,7 @@
             VMEM((half, fw), bf16), VMEM((half, rank), bf16),
             VMEM((panels, split - 1, piece, width), bf16),
             VMEM((panels, layers - 1, piece, width), bf16),
-            VMEM((panels, piece, width), bf16),
+            VMEM((panels, piece, width), bf16), VMEM((panels, (layers - 1).bit_length(), piece, width), bf16),
             VMEM((panels, size, count), bf16),
             VMEM((panels, size, size), f32), VMEM((panels, size, size), f32),
             VMEM((size, size), f32), VMEM((size, size), f32), VMEM((half, size), f32),

time: 62.3 us -> 60.1 us (0.965)
  the two profiles are of different devices: /device:TPU:1 before, /device:TPU:0 now
where the time goes in v3:
time: 60.1 us; the launch traced here: 59.9 us
  Pallas kernels  59.1 us (98%)
  between operations  0.8 us (1%)
    pallas_call x1, Pallas kernels, body(): pl.pallas_call(functools.partial(panel_kernel, split, layers, scale), out...  58.2 us

profile of v3, /device:TPU:0, one launch (start us, length us, event | category | flops | bytes accessed | tf_op | source)
XLA Modules:
  0.0 59.9 jit_solution(13407029410960369661)
XLA Ops:
  0.6 58.2 %panels.1 = (bf16[1280,256]{1,0:T(8,128)(2,1)S(1)}, f32[32,512]{1,0:T(8,128)S(1)}, f32[32,256]{1,0:T(8,128)S(1)}) custom-call(s32[4,128]{1,0:T(4,128)} %slots.1, s32[4,128]{1,0:T(4,128)} %owners.1, bf16[1280,256]{1,0:T(8,128)(2,1)} %points_in.1, bf16[1280,512]{1,0:T(8,128)(2,1)} %factor_in.1, f32[10,128]{1,0:T(8,128)} %bitcast.1), custom_call_target="tpu_custom_call" | custom-call | tf_op jit(solution)/shard_map/panels/pallas_call | solution.py:620
  58.8 0.9 %write.1 = (bf16[1280,256]{1,0:T(8,128)(2,1)}, f32[32,512]{1,0:T(8,128)}, f32[32,256]{1,0:T(8,128)}) custom-call(bf16[1280,256]{1,0:T(8,128)(2,1)S(1)} %get-tuple-element.6.a, f32[32,512]{1,0:T(8,128)S(1)} %get-tuple-element.7.b, f32[32,256]{1,0:T(8,128)S(1)} %get-tuple-element.8.c), custom_call_target="tpu_custom_call" | custom-call | tf_op jit(solution)/shard_map/write/pallas_call | solution.py:657

commit v4 on v3

--- a/solution.py
+++ b/solution.py
@@ -11,6 +11,7 @@
 RIDGE_LEVEL = 1.0
 BLOCK = 8
 HOOKS = (4, 8, 10, 12, 14)
+PLACES = (0, 1, 1, 3, 4)
 VMEM = pltpu.VMEM
 HIGH = lax.Precision.HIGHEST
 NT = (((1,), (1,)), ((), ()))
@@ -122,7 +123,7 @@
                  ga_send, ga_recv, gb_send, gb_recv, na_send, na_recv, nb_send, nb_recv,
                  ca_send, ca_recv, cb_send, cb_recv,
                  points, factor, load, part, piv, other_points, other_factor, buf_a, buf_b, acc, mid,
-                 prow, inv, norms, early, ready, columns, rows, wide,
+                 prow, inv, norms, early, ready, columns, levels, rows, wide,
                  a_send, a_recv, b_send, b_recv, f_send, f_recv,
                  d_send, d_recv, e_send, e_recv, x_send, x_recv):
     me = lax.axis_index("rows")
@@ -194,9 +195,9 @@
         source = mid.at[q, j - 1] if j else acc.at[q]
         return remote(source, buf_b.at[q, j], b_send.at[q, j], b_recv.at[q, j], away * inner + place, col)
 
-    def sends_b(q):
+    def sends_b(q, count=None):
         if q and paired:
-            return [twice(q, j) for j in range(steps)]
+            return [twice(q, j) for j in range(count or steps)]
         return [along(q, d) for d in range(1, outer)]
 
     def layer_sum(q):
@@ -205,7 +206,7 @@
             within(q, d).wait_recv()
             total = total + buf_a[q, d - 1]
         acc[q] = total
-        for c in sends_b(q)[:1 if q and paired else outer]:
+        for c in sends_b(q, 1):
             c.start()
 
     def between(q):
@@ -279,6 +280,9 @@
     same = lax.broadcasted_iota(jnp.int32, (size, size), 0) == lax.broadcasted_iota(jnp.int32, (size, size), 1)
     eye = jnp.where(same, 1.0, 0.0)
 
+    for i in range(here // size):
+        levels[i * size:(i + 1) * size, :] = turned(weights[i:i + 1, :])
+
     whole_sum(0)
     for q in range(2, panels):
         between(q)
@@ -370,9 +374,8 @@
 
         def part_of(source, which):
             for i in range(half // size):
-                level = turned(weights[pl.ds(which * (half // size) + i, 1), :])[:, 0:1]
-                block = source[i * size:(i + 1) * size, lanes].astype(f32) * level
                 first = pl.multiple_of(which * half + i * size, size)
+                block = source[i * size:(i + 1) * size, lanes].astype(f32) * levels[pl.ds(first, size), :]
                 level_t[lanes, pl.ds(first, size)] = jnp.transpose(block).astype(bf16)
             spots = pl.ds(pl.multiple_of(which * half, size), half)
             return jnp.dot(level_t[lanes, spots], factor[half_rows(which), :], preferred_element_type=f32)
@@ -439,11 +442,15 @@
     def solve(r):
         out_ref[:, span(r)] = exact(columns[...], inv[r]).astype(bf16)
 
-    def fill(r):
+    def fill(r, place_of):
         ids = owners[r:r + 1, :] * here + slots[r:r + 1, :]
-        value = entries(points[mine, :], other_points[...], factor[mine, :], other_factor[...], r, own_norm)
-        value = value + jnp.where(own_ids == ids, RIDGE_LEVEL, 0.0)
-        columns[...] = less(value, out_ref, prow[r], r)
+        blocks = half // size
+        for i in [i for i in range(blocks) if PLACES[i * len(PLACES) // blocks] == place_of]:
+            own = pl.ds(pl.multiple_of(col * half + i * size, 16), size)
+            value = entries(points[own, :], other_points[span(i), :], factor[own, :], other_factor[span(i), :], r,
+                            own_norm[span(i), :])
+            value = value + jnp.where(own_ids[span(i), :] == ids, RIDGE_LEVEL, 0.0)
+            columns[span(i), :] = less(value, out_ref.at[span(i)], prow[r], r)
 
     arrive(0)
     head(0)
@@ -455,12 +462,14 @@
                 whole_sum(2)
             if q == 1:
                 forward(2)
+            fill(q, 1)
 
         def hook_b():
             if q > 0:
                 gram_block(q - 1)
             if q == panels - 1:
                 new_early()
+            fill(q, 2)
 
         def hook_c():
             if q == 0:
@@ -469,6 +478,7 @@
             elif q + 1 < panels:
                 arrive(q + 1)
                 head(q + 1)
+            fill(q, 3)
 
         def hook_d():
             if q > 0:
@@ -478,6 +488,7 @@
                     new_a(0, d).start()
             if q == 1:
                 forward(3)
+            fill(q, 4)
 
         def hook_e():
             if q == 0:
@@ -489,8 +500,8 @@
         begin(q)
         if q:
             solve(q - 1)
-        fill(q)
-        hooks = dict(zip((at * BLOCK for at in HOOKS), (hook_a, hook_b, hook_c, hook_d, hook_e)))
+        fill(q, 0)
+        hooks = dict(zip((at * size // 16 for at in HOOKS), (hook_a, hook_b, hook_c, hook_d, hook_e)))
         factor_block(size, inv.at[q], rows, wide, hooks)
     solve(panels - 1)
     swap_panel(panels - 1).start()
@@ -647,6 +658,7 @@
             VMEM((panels, size, count), bf16),
             VMEM((panels, size, size), f32), VMEM((panels, size, size), f32),
             VMEM((size, size), f32), VMEM((size, size), f32), VMEM((half, size), f32),
+            VMEM((here, size), f32),
             VMEM((4 * BLOCK, size), f32), VMEM((6 * BLOCK, BLOCK, size), f32),
             sem(panels, split - 1), sem(panels, split - 1), sem(panels, layers - 1), sem(panels, layers - 1),
             sem(panels), sem(panels), sem(panels, split - 1), sem(panels, split - 1),

time: 60.1 us -> 58.6 us (0.975)
  Pallas kernels: 59.1 us -> 57.6 us
    pallas_call x1, Pallas kernels: 58.2 us -> 56.7 us  [body(): pl.pallas_call(functools.partial(panel_kernel, split, layers, scale), out...]
where the time goes in v4:
time: 58.6 us; the launch traced here: 58.4 us
  Pallas kernels  57.6 us (98%)
  between operations  0.8 us (1%)
    pallas_call x1, Pallas kernels, body(): pl.pallas_call(functools.partial(panel_kernel, split, layers, scale), out...  56.7 us

profile of v4, /device:TPU:0, one launch (start us, length us, event | category | flops | bytes accessed | tf_op | source)
XLA Modules:
  0.0 58.4 jit_solution(13824601926135802620)
XLA Ops:
  0.6 56.7 %panels.1 = (bf16[1280,256]{1,0:T(8,128)(2,1)S(1)}, f32[32,512]{1,0:T(8,128)S(1)}, f32[32,256]{1,0:T(8,128)S(1)}) custom-call(s32[4,128]{1,0:T(4,128)} %slots.1, s32[4,128]{1,0:T(4,128)} %owners.1, bf16[1280,256]{1,0:T(8,128)(2,1)} %points_in.1, bf16[1280,512]{1,0:T(8,128)(2,1)} %factor_in.1, f32[10,128]{1,0:T(8,128)} %bitcast.1), custom_call_target="tpu_custom_call" | custom-call | tf_op jit(solution)/shard_map/panels/pallas_call | solution.py:631
  57.3 0.9 %write.1 = (bf16[1280,256]{1,0:T(8,128)(2,1)}, f32[32,512]{1,0:T(8,128)}, f32[32,256]{1,0:T(8,128)}) custom-call(bf16[1280,256]{1,0:T(8,128)(2,1)S(1)} %get-tuple-element.6.a, f32[32,512]{1,0:T(8,128)S(1)} %get-tuple-element.7.b, f32[32,256]{1,0:T(8,128)S(1)} %get-tuple-element.8.c), custom_call_target="tpu_custom_call" | custom-call | tf_op jit(solution)/shard_map/write/pallas_call | solution.py:669
